TPU v7x, 32 devices: a whole 2x2x4 slice. The times are simulated.
32 devices in a mesh: parts: 2 (over y), ctx: 4 (over z), head: 2 (over x), sub: 2 (over core).
Axes of the slice: x: 2, y: 2, z: 4, core: 2. Of those that a mesh axis runs over, the one named last changes fastest.
Arguments:
- queries: bfloat16 [4096, 4096], P(('parts', 'ctx', 'head', 'sub')), parts along dimension 0, may hold values from -6 to 6
- keys: bfloat16 [4096, 4096], P(('parts', 'ctx', 'head', 'sub')), parts along dimension 0, may hold values from -6 to 6
- values: bfloat16 [4096, 4096], P(('parts', 'ctx', 'head', 'sub')), parts along dimension 0, may hold values from -6 to 6
Outputs:
- attended: bfloat16 [4096, 4096], P(('parts', 'ctx', 'head', 'sub')), parts along dimension 0
There are 2 independent parts, one for each index of `parts`. A program takes and returns all parts, laid end to end along the dimension named above; each array names one. Nothing has to cross between parts.
All inputs are finite; a program needn't handle non-finite values.
Results may differ from a plain program's by a relative error of at most 0.006.
Values may be sent and summed in bfloat16 or wider, within the bound.
A program may use at most 64 MiB of HBM per device.

v0:
```python
import jax
import jax.numpy as jnp
from jax import lax
from jax.sharding import PartitionSpec as P

HEADS = 32
HD = 128


def prefix_2(array, axis, join, neutral):
    place = lax.axis_index(axis)
    gathered = lax.all_gather(array.astype(jnp.bfloat16), axis)
    state = jnp.zeros_like(array) + jnp.asarray(neutral, array.dtype)

    def one(turn, state):
        return join(state, lax.dynamic_index_in_dim(gathered, turn, 0, False).astype(array.dtype))

    return lax.fori_loop(0, place, one, state)


def feature(x):
    return (jax.nn.elu(x.astype(jnp.float32)) + 1.0).astype(jnp.bfloat16)


def block_count(total_rows):
    return total_rows // 128


def block_states(phi_k, vals, blocks):
    total_rows, heads, width = phi_k.shape
    span = total_rows // blocks
    kb = phi_k.reshape(blocks, span, heads, width)
    vb = vals.reshape(blocks, span, heads, width)
    return jnp.einsum("nbhd,nbhe->nhde", kb, vb, preferred_element_type=jnp.float32)


def finish(phi_q, phi_k, vals, states, prefix):
    blocks = states.shape[0]
    total_rows, heads, width = phi_q.shape
    span = total_rows // blocks
    qb = phi_q.reshape(blocks, span, heads, width)
    kb = phi_k.reshape(blocks, span, heads, width)
    vb = vals.reshape(blocks, span, heads, width)
    earlier = jnp.cumsum(states, axis=0) - states + prefix[None]
    inter = jnp.einsum(
        "nbhd,nhde->nbhe", qb.astype(jnp.float32), earlier, precision=lax.Precision.HIGHEST
    )
    scores = jnp.einsum("nbhd,nchd->nhbc", qb, kb, preferred_element_type=jnp.float32)
    causal = jnp.tril(jnp.ones((span, span), jnp.float32))
    scores = scores * causal
    upper = scores.astype(jnp.bfloat16)
    lower = (scores - upper.astype(jnp.float32)).astype(jnp.bfloat16)
    intra = jnp.einsum("nhbc,nche->nbhe", upper, vb, preferred_element_type=jnp.float32)
    intra = intra + jnp.einsum("nhbc,nche->nbhe", lower, vb, preferred_element_type=jnp.float32)
    numer = (inter + intra).reshape(total_rows, heads, width)
    scaled = numer * lax.rsqrt(jnp.mean(numer * numer, axis=-1, keepdims=True) + 1e-06)
    return scaled.astype(jnp.bfloat16)


def add_states(earlier, later):
    return earlier + later


def body(queries, keys, values):
    tok_rows = queries.shape[0]
    phi_q = feature(queries).reshape(tok_rows, HEADS, HD)
    phi_k = feature(keys).reshape(tok_rows, HEADS, HD)
    vals = values.reshape(tok_rows, HEADS, HD)
    phi_q, phi_k, vals = (
        lax.all_to_all(phi_q, ("head", "sub"), split_axis=1, concat_axis=0, tiled=True),
        lax.all_to_all(phi_k, ("head", "sub"), split_axis=1, concat_axis=0, tiled=True),
        lax.all_to_all(vals, ("head", "sub"), split_axis=1, concat_axis=0, tiled=True),
    )
    local_rows = phi_q.shape[0]
    states = block_states(phi_k, vals, block_count(local_rows))
    device_total = jnp.sum(states, axis=0)
    prefix = prefix_2(device_total, "ctx", add_states, jnp.zeros_like(device_total))
    scaled = finish(phi_q, phi_k, vals, states, prefix)
    scaled = lax.all_to_all(scaled, ("head", "sub"), split_axis=0, concat_axis=1, tiled=True)
    return scaled.reshape(tok_rows, HEADS * HD)


def solution(mesh):
    return jax.shard_map(
        body,
        mesh=mesh,
        in_specs=(
            P(("parts", "ctx", "head", "sub"), None),
            P(("parts", "ctx", "head", "sub"), None),
            P(("parts", "ctx", "head", "sub"), None),
        ),
        out_specs=P(("parts", "ctx", "head", "sub"), None),
        check_vma=False,
    )
```

profile of v0, /device:TPU:29, one launch (start us, length us, event | category | flops | bytes accessed | tf_op | source)
XLA Modules:
  0.0 118.0 jit_solution(8116780801651236212)
XLA Ops:
  6.5 0.0 copy-start
  6.5 2.2 %fusion.2 = bf16[128,4096]{1,0:T(8,128)(2,1)S(1)} fusion(bf16[128,4096]{1,0:T(8,128)(2,1)} %param.6), kind=kLoop, calls=%fused_computation.7 | loop fusion | flops 3145728 | bytes 2097152 | tf_op jit(solution)/shard_map/convert_element_type | solution.py:22
  8.8 1.3 %copy.36 = bf16[128,4096]{0,1:T(8,128)(2,1)} copy(bf16[128,4096]{1,0:T(8,128)(2,1)S(1)} %fusion.2) | data formatting | bytes 2097152 | tf_op jit(solution)/shard_map/reshape | solution.py:67
  10.1 4.2 %all-to-all-start = ((bf16[128,32,128]{0,2,1:T(8,128)(2,1)}), bf16[128,32,128]{0,2,1:T(8,128)(2,1)S(1)}, u32[]{:S(2)}, u32[]{:S(2)}) async-start(bf16[128,32,128]{0,2,1:T(8,128)(2,1)} %bitcast.1), calls=%async_computation | async-start | bytes 2097152 | tf_op jit(solution)/shard_map/all_to_all | solution.py:71
  14.2 0.0 copy-done
  14.2 1.3 %copy_bitcast_fusion.1 = bf16[128,32,128]{2,0,1:T(8,128)(2,1)} fusion(bf16[128,4096]{1,0:T(8,128)(2,1)S(1)} %copy-done), kind=kLoop, calls=%fused_computation.24 | loop fusion | bytes 2097152 | tf_op jit(solution)/shard_map/reshape | solution.py:68
  15.5 12.2 %all-to-all-done = bf16[128,32,128]{0,2,1:T(8,128)(2,1)S(1)} async-done(((bf16[128,32,128]{0,2,1:T(8,128)(2,1)}), bf16[128,32,128]{0,2,1:T(8,128)(2,1)S(1)}, u32[]{:S(2)}, u32[]{:S(2)}) %all-to-all-start) | async-done | bytes 1048608 | tf_op jit(solution)/shard_map/all_to_all | solution.py:71
  27.7 0.0 copy-start.4
  27.7 4.5 %all-to-all-start.1 = ((bf16[128,32,128]{2,0,1:T(8,128)(2,1)}), bf16[128,32,128]{2,0,1:T(8,128)(2,1)S(1)}, u32[]{:S(2)}, u32[]{:S(2)}) async-start(bf16[128,32,128]{2,0,1:T(8,128)(2,1)} %copy_bitcast_fusion.1), calls=%async_computation.1 | async-start | bytes 2097152 | tf_op jit(solution)/shard_map/all_to_all | solution.py:72
  32.2 3.2 %copy_bitcast_fusion = bf16[128,32,128]{2,0,1:T(8,128)(2,1)} fusion(bf16[128,4096]{1,0:T(8,128)(2,1)} %param.5), kind=kLoop, calls=%fused_computation.23 | loop fusion | flops 3145728 | bytes 2097152 | tf_op jit(solution)/shard_map/reshape | solution.py:66
  35.3 10.3 %all-to-all-done.1 = bf16[128,32,128]{2,0,1:T(8,128)(2,1)S(1)} async-done(((bf16[128,32,128]{2,0,1:T(8,128)(2,1)}), bf16[128,32,128]{2,0,1:T(8,128)(2,1)S(1)}, u32[]{:S(2)}, u32[]{:S(2)}) %all-to-all-start.1) | async-done | bytes 1048608 | tf_op jit(solution)/shard_map/all_to_all | solution.py:72
  45.6 0.0 copy-start.2
  45.6 0.0 copy-done.4
  45.6 5.2 %all-to-all-start.2 = ((bf16[128,32,128]{2,0,1:T(8,128)(2,1)}), bf16[128,32,128]{2,0,1:T(8,128)(2,1)}, u32[]{:S(2)}, u32[]{:S(2)}) async-start(bf16[128,32,128]{2,0,1:T(8,128)(2,1)} %copy_bitcast_fusion), calls=%async_computation.2 | async-start | bytes 2097152 | tf_op jit(solution)/shard_map/all_to_all | solution.py:70
  50.8 0.0 all-gather.3.cloned.1.call-start
  50.8 0.0 copy-done.2
  50.8 2.7 %fusion.19 = (bf16[8,128,128]{2,1,0:T(8,128)(2,1)}, f32[4,8,128,128]{3,2,1,0:T(8,128)S(1)}) fusion(bf16[4,128,8,128]{1,3,2,0:T(8,128)(2,1)} %bitcast.51, bf16[4,128,8,128]{3,1,2,0:T(8,128)(2,1)} %bitcast.48), kind=kOutput, calls=%fused_computation.31 | convolution fusion | flops 134610944 | bytes 4456448 | tf_op jit(solution)/shard_map/nbhd,nbhe->nhde/dot_general | solution.py:34
  53.6 0.0 copy-start.1
  53.6 0.0 all-gather.3.cloned.1.call-update
  53.6 10.8 %all-to-all-done.2 = bf16[128,32,128]{2,0,1:T(8,128)(2,1)} async-done(((bf16[128,32,128]{2,0,1:T(8,128)(2,1)}), bf16[128,32,128]{2,0,1:T(8,128)(2,1)}, u32[]{:S(2)}, u32[]{:S(2)}) %all-to-all-start.2) | async-done | bytes 1048608 | tf_op jit(solution)/shard_map/all_to_all | solution.py:70
  64.4 2.0 %fusion.21 = f32[4,8,128,128]{3,2,1,0:T(8,128)S(1)} fusion(bf16[4,128,8,128]{3,1,2,0:T(8,128)(2,1)} %bitcast.8, bf16[4,128,8,128]{1,3,2,0:T(8,128)(2,1)} %bitcast.52), kind=kOutput, calls=%fused_computation.33 | convolution fusion | flops 134217728 | bytes 4194304 | tf_op jit(solution)/shard_map/nbhd,nchd->nhbc/dot_general | solution.py:48
  66.4 0.0 copy-done.1
  66.4 0.0 copy-start.3
  66.4 1.5 %fusion.20 = f32[4,8,128,128]{3,2,1,0:T(8,128)} fusion(f32[4,8,128,128]{3,2,1,0:T(8,128)S(1)} %get-tuple-element.38), kind=kOutput, calls=%fused_computation.32 | output fusion | flops 1572864 | bytes 4194304 | tf_op jit(solution)/shard_map/jit(cumsum)/reduce_window_sum | solution.py:44
  67.9 0.0 copy-done.3
  67.9 1.7 %fusion.12 = f32[4,8,128,128]{3,2,1,0:T(8,128)} fusion(bf16[4,128,8,128]{3,1,2,0:T(8,128)(2,1)S(1)} %bitcast.49, f32[4,8,128,128]{3,2,1,0:T(8,128)S(1)} %fusion.21, f32[128,128]{1,0:T(8,128)S(1)} %fusion.18), kind=kOutput, calls=%fused_computation.20 | convolution fusion | flops 135266304 | bytes 5308416 | tf_op jit(solution)/shard_map/nhbc,nche->nbhe/dot_general | solution.py:53
  69.7 1.8 %fusion.13 = f32[4,8,128,128]{3,2,1,0:T(8,128)} fusion(bf16[4,128,8,128]{3,1,2,0:T(8,128)(2,1)S(1)} %bitcast.50, f32[4,8,128,128]{3,2,1,0:T(8,128)S(1)} %fusion.21, f32[128,128]{1,0:T(8,128)S(1)} %fusion.18), kind=kOutput, calls=%fused_computation.21 | convolution fusion | flops 136839168 | bytes 5308416 | tf_op jit(solution)/shard_map/nhbc,nche->nbhe/dot_general | solution.py:54
  71.4 9.6 %all-gather.3.cloned.1.call-done = bf16[32,128,128]{2,1,0:T(8,128)(2,1)} async-done(((bf16[8,128,128]{2,1,0:T(8,128)(2,1)}), bf16[32,128,128]{2,1,0:T(8,128)(2,1)}) %all-gather.3.cloned.1.call-update) | async-done | bytes 1048592 | tf_op jit(solution)/shard_map/all_gather | solution.py:12
  81.1 3.3 %while.10 = (s32[]{:T(128)}, f32[8,128,128]{2,1,0:T(8,128)S(1)}, s32[]{:T(128)}, bf16[4,8,128,128]{3,2,1,0:T(8,128)(2,1)}, s32[]{:T(128)}, /*index=5*/s32[]{:T(128)}, s32[]{:T(128)}) while((s32[]{:T(128)}, f32[8,128,128]{2,1,0:T(8,128)S(1)}, s32[]{:T(128)}, bf16[4,8,128,128]{3,2,1,0:T(8,128)(2,1)}, s32[]{:T(128)}, /*index=5*/s32[]{:T(128)}, ...), condition=%wide.region_3.4_spmd, body=%wide.region_2.3_spmd.sunk | while | flops 262149 | bytes 1310835 | solution.py:18
  81.2 1.1 convert_add_fusion.2
  82.3 1.1 convert_add_fusion.2
  83.3 1.1 convert_add_fusion.2
  84.4 5.9 %multiply_reduce_fusion = (f32[4,128,8]{1,2,0:T(8,128)S(1)}, f32[4,128,8,128]{3,1,2,0:T(8,128)S(1)}) fusion(f32[4,8,128,128]{3,2,1,0:T(8,128)} %fusion.12, f32[4,8,128,128]{3,2,1,0:T(8,128)} %fusion.13, bf16[4,128,8,128]{3,1,2,0:T(8,128)(2,1)} %bitcast.8, f32[4,8,128,128]{3,2,1,0:T(8,128)} %fusion.20, f32[4,8,128,128]{3,2,1,0:T(8,128)} %copy-done.1, ...), kind=kOutput, calls=%fused_computation.14 | convolution fusion | flops 808448000 | bytes 12075008 | tf_op jit(solution)/shard_map/nbhd,nhde->nbhe/dot_general | solution.py:45
  90.3 1.2 %copy.31 = f32[4,128,8,128]{3,2,1,0:T(8,128)S(1)} copy(f32[4,128,8,128]{3,1,2,0:T(8,128)S(1)} %get-tuple-element.40) | data formatting | bytes 4194304 | tf_op jit(solution)/shard_map/add | solution.py:55
  91.6 0.1 copy.32
  91.7 0.9 fusion.6
  92.6 16.5 %all_to_all.60 = bf16[512,8,128]{2,1,0:T(8,128)(2,1)S(1)} all-to-all(bf16[512,8,128]{2,1,0:T(8,128)(2,1)S(1)} %fusion.6), channel_id=1, replica_groups=mesh['parts'=2,'ctx'=4,'head'=2,'sub'=2] {'head','sub'}, dimensions={0} | all-to-all | bytes 2097152 | tf_op jit(solution)/shard_map/all_to_all | solution.py:79
  109.1 0.8 copy.33
  109.9 1.3 %copy.34 = bf16[128,4096]{1,0:T(8,128)(2,1)} copy(bf16[128,4096]{0,1:T(8,128)(2,1)S(1)} %bitcast.54) | data formatting | bytes 2097152 | tf_op jit(solution)/shard_map/reshape | solution.py:80
  (3 shorter events, 0.1 us)
Async XLA Ops:
  6.5 7.7 %copy-start = (bf16[128,4096]{1,0:T(8,128)(2,1)S(1)}, bf16[128,4096]{1,0:T(8,128)(2,1)}, u32[]{:S(2)}) copy-start(bf16[128,4096]{1,0:T(8,128)(2,1)} %param.7) | copy-start | bytes 3145732
  10.1 17.6 %all-to-all-start = ((bf16[128,32,128]{0,2,1:T(8,128)(2,1)}), bf16[128,32,128]{0,2,1:T(8,128)(2,1)S(1)}, u32[]{:S(2)}, u32[]{:S(2)}) async-start(bf16[128,32,128]{0,2,1:T(8,128)(2,1)} %bitcast.1), calls=%async_computation | async-start | bytes 2097152 | tf_op jit(solution)/shard_map/all_to_all | solution.py:71
  27.7 17.9 %copy-start.4 = (bf16[128,32,128]{0,2,1:T(8,128)(2,1)}, bf16[128,32,128]{0,2,1:T(8,128)(2,1)S(1)}, u32[]{:S(2)}) copy-start(bf16[128,32,128]{0,2,1:T(8,128)(2,1)S(1)} %all-to-all-done) | copy-start | bytes 3145732
  27.7 17.9 %all-to-all-start.1 = ((bf16[128,32,128]{2,0,1:T(8,128)(2,1)}), bf16[128,32,128]{2,0,1:T(8,128)(2,1)S(1)}, u32[]{:S(2)}, u32[]{:S(2)}) async-start(bf16[128,32,128]{2,0,1:T(8,128)(2,1)} %copy_bitcast_fusion.1), calls=%async_computation.1 | async-start | bytes 2097152 | tf_op jit(solution)/shard_map/all_to_all | solution.py:72
  45.6 5.2 %copy-start.2 = (bf16[128,32,128]{2,0,1:T(8,128)(2,1)}, bf16[128,32,128]{2,0,1:T(8,128)(2,1)S(1)}, u32[]{:S(2)}) copy-start(bf16[128,32,128]{2,0,1:T(8,128)(2,1)S(1)} %all-to-all-done.1) | copy-start | bytes 3145732
  45.6 18.8 %all-to-all-start.2 = ((bf16[128,32,128]{2,0,1:T(8,128)(2,1)}), bf16[128,32,128]{2,0,1:T(8,128)(2,1)}, u32[]{:S(2)}, u32[]{:S(2)}) async-start(bf16[128,32,128]{2,0,1:T(8,128)(2,1)} %copy_bitcast_fusion), calls=%async_computation.2 | async-start | bytes 2097152 | tf_op jit(solution)/shard_map/all_to_all | solution.py:70
  50.8 30.3 %all-gather.3.cloned.1.call-start = ((), (), s32[]{:S(2)}) async-start(), calls=%async_computation.4 | async-start | bytes 1310720 | tf_op jit(solution)/shard_map/all_gather | solution.py:12
  53.6 12.8 %copy-start.1 = (f32[4,8,128,128]{3,2,1,0:T(8,128)}, f32[4,8,128,128]{3,2,1,0:T(8,128)S(1)}, u32[]{:S(2)}) copy-start(f32[4,8,128,128]{3,2,1,0:T(8,128)S(1)} %get-tuple-element.38) | copy-start | bytes 6291460
  66.4 1.5 %copy-start.3 = (bf16[128,32,128]{2,0,1:T(8,128)(2,1)S(1)}, bf16[128,32,128]{2,0,1:T(8,128)(2,1)}, u32[]{:S(2)}) copy-start(bf16[128,32,128]{2,0,1:T(8,128)(2,1)} %copy-done.2) | copy-start | bytes 3145732
Sparse Core Ops, SparseCore 0:
  53.7 27.3 all-gather.2
where the time goes:
time: 119 us; the launch traced here: 118 us
  waiting for transfers between devices  43 us (36%)
  blocking collectives  16.5 us (14%)
  matrix products  14.1 us (12%)
  starting transfers between devices  13.8 us (12%)
  between operations  13.5 us (11%)
  other arithmetic  11 us (9%)
  local copies, waits for them, and re-layouts  6.07 us (5%)
    all_to_all x1, blocking collectives, body(): lax.all_to_all(scaled, ('head', 'sub'), split_axis=0, concat_axis=1, tile...  16.5 us
    all_to_all x1, waiting for transfers between devices, body(): lax.all_to_all(phi_k, ('head', 'sub'), split_axis=1, concat_axis=0, tiled...  12.2 us
    all_to_all x1, waiting for transfers between devices, body(): lax.all_to_all(phi_q, ('head', 'sub'), split_axis=1, concat_axis=0, tiled...  10.8 us
    all_to_all x1, waiting for transfers between devices, body(): lax.all_to_all(vals, ('head', 'sub'), split_axis=1, concat_axis=0, tiled=...  10.3 us
    all_gather x1, waiting for transfers between devices, prefix_2(): gathered = lax.all_gather(array.astype(jnp.bfloat16), axis)  9.64 us
    dot_general x1, matrix products, finish(): jnp.einsum('nbhd,nhde->nbhe', qb.astype(jnp.float32), earlier, precision=...  5.88 us
    all_to_all x1, starting transfers between devices, body(): lax.all_to_all(phi_q, ('head', 'sub'), split_axis=1, concat_axis=0, tiled...  5.19 us
    all_to_all x1, starting transfers between devices, body(): lax.all_to_all(vals, ('head', 'sub'), split_axis=1, concat_axis=0, tiled=...  4.46 us
  transfers between devices with their start and end apart: 4, of which 4 were waited for; matrix products, arithmetic and copies ran while one was open for 12% of the time, Pallas kernels for 0%

commit v1 on v0

v1 whole, which is shorter than its diff:
```python
import functools

import jax
import jax.numpy as jnp
from jax import lax
from jax.experimental import pallas as pl
from jax.experimental.pallas import tpu as pltpu
from jax.sharding import PartitionSpec as P

HEADS = 32
HD = 128
HALF = HEADS // 2
MESH = pl.DeviceIdType.MESH
F32 = jnp.float32
BF16 = jnp.bfloat16


def phi(x):
    x = x.astype(F32)
    return jnp.where(x > 0.0, x + 1.0, jnp.exp(x)).astype(BF16)


def lanes(head, count=1):
    return pl.ds(pl.multiple_of(head * HD, HD), count * HD)


def kernel(
    nx, nz, hp, lag,
    q_hbm, k_hbm, v_hbm, o_hbm,
    qv, kv, vv, kphi, qphi, numer, outv,
    s_par, s_own, e1_recv, t_send, t_recv, z_send, z_recv, q_send, q_recv,
    c_send, c_recv, p_own,
    ld_sem, out_sem, e_ss, e_rs, t_ss, t_rs, z_ss, z_rs, q_ss, q_rs, c_ss, c_rs,
):
    rows = qv.shape[0]
    x = lax.axis_index("head")
    z = lax.axis_index("ctx")
    c = lax.axis_index("sub")
    other = 1 - c

    barrier = pltpu.get_barrier_semaphore()

    def greet(**where):
        pl.semaphore_signal(barrier, inc=1, device_id=where, device_id_type=MESH)

    greet(sub=other)
    for d in range(1, nx):
        greet(head=lax.rem(x + d, nx))

    @pl.when(z > 0)
    def _():
        greet(ctx=z - 1)

    @pl.when(z < nz - 1)
    def _():
        greet(ctx=z + 1)

    def column(u):
        return lax.rem(x + 1 + u, nx)

    def loads(u):
        out = []
        for w in range(2):
            base = (other if w == 0 else c) * HALF + column(u) * hp
            at = lanes(base, hp)
            for m, (src, dst) in enumerate(((k_hbm, kv), (v_hbm, vv))):
                out.append(
                    pltpu.make_async_copy(
                        src.at[:, at], dst.at[:, at], ld_sem.at[u * 4 + w * 2 + m]
                    )
                )
        return out

    for u in range(nx):
        for copy in loads(u):
            copy.start()
    q_load = pltpu.make_async_copy(q_hbm, qv, ld_sem.at[4 * nx])
    q_load.start()

    @pl.when(z == 0)
    def _():
        z_recv[...] = jnp.zeros_like(z_recv)

    def remote(src, dst, ss, rs, **where):
        return pltpu.make_async_remote_copy(
            src_ref=src, dst_ref=dst, send_sem=ss, recv_sem=rs,
            device_id=where, device_id_type=MESH,
        )

    def e_copy(o):
        return remote(s_par.at[o], e1_recv.at[o], e_ss.at[o], e_rs.at[o], sub=other)

    def t_copy(o, col, j):
        return remote(
            t_send.at[o], t_recv.at[x, j], t_ss.at[o], t_rs.at[x * hp + j], head=col
        )

    def t_wait(xs, j):
        remote(
            t_recv.at[xs, j], t_recv.at[xs, j], t_ss.at[0], t_rs.at[xs * hp + j], head=xs
        ).wait_recv()

    def z_copy(j, to):
        return remote(z_send.at[j], z_recv.at[j], z_ss.at[j], z_rs.at[j], ctx=to)

    def q_copy(o, xt, j):
        return remote(
            q_send.at[xt, j], q_recv.at[o], q_ss.at[xt * hp + j], q_rs.at[o], head=xt
        )

    def c_copy(o):
        return remote(c_send.at[o], c_recv.at[o], c_ss.at[o], c_rs.at[o], sub=other)

    up = jnp.where(z < nz - 1, 1, 0)
    down = jnp.where(z > 0, 1, 0)
    pl.semaphore_wait(barrier, nx + up + down)

    def own_index(t):
        u = t // hp
        j = lax.rem(t, hp)
        col = column(u)
        return col * hp + j, col, j

    def first_sums(t):
        o, col, j = own_index(t)
        e_copy(o).wait_recv()
        t_send[o] = (s_own[o].astype(F32) + e1_recv[o].astype(F32)).astype(BF16)
        t_copy(o, col, j).start()

    first_count = (nx - 1) * hp

    def state_step(t, carry):
        o, col, j = own_index(t)
        for u in range(nx):

            @pl.when(t == u * hp)
            def _():
                for copy in loads(u):
                    copy.wait()

        for w in range(2):
            at = lanes((other if w == 0 else c) * HALF + o)
            pk = phi(kv[:, at])
            kphi[:, at] = pk
            s = lax.dot_general(
                pk, vv[:, at], (((0,), (0,)), ((), ())), preferred_element_type=F32
            ).astype(BF16)
            if w == 0:
                s_par[o] = s
            else:
                s_own[o] = s
        e_copy(o).start()

        @pl.when((t >= lag) & (t - lag < first_count))
        def _():
            first_sums(t - lag)

        return carry

    lax.fori_loop(0, HALF, state_step, 0)

    def rest(t, carry):
        first_sums(t)
        return carry

    lax.fori_loop(max(HALF - lag, 0), first_count, rest, 0)

    q_load.wait()
    row = lax.broadcasted_iota(jnp.int32, (rows, rows), 0)
    colm = lax.broadcasted_iota(jnp.int32, (rows, rows), 1)
    causal = row >= colm

    def local_step(g, carry):
        for i in range(4):
            at = lanes(g * 4 + i)
            pq = phi(qv[:, at])
            qphi[:, at] = pq
            scores = lax.dot_general(
                pq, kphi[:, at], (((1,), (1,)), ((), ())), preferred_element_type=F32
            )
            scores = jnp.where(causal, scores, 0.0).astype(BF16)
            numer[:, at] = jnp.dot(scores, vv[:, at], preferred_element_type=F32)
        return carry

    def local_all():
        lax.fori_loop(0, HEADS // 4, local_step, 0)

    early = z >= (nz + 1) // 2

    @pl.when(early)
    def _():
        local_all()

    def deliver(o, before):
        @pl.when(c == 0)
        def _():
            p_own[o] = before.astype(BF16)
            c_send[o] = (before + s_own[o].astype(F32)).astype(BF16)

        @pl.when(c == 1)
        def _():
            c_send[o] = before.astype(BF16)
            p_own[o] = (before + e1_recv[o].astype(F32)).astype(BF16)

        c_copy(o).start()

    def chain(j):
        o = x * hp + j
        e_copy(o).wait_recv()
        t_recv[x, j] = (s_own[o].astype(F32) + e1_recv[o].astype(F32)).astype(BF16)
        for d in range(1, nx):
            t_wait(lax.rem(x + d, nx), j)

        @pl.when(z > 0)
        def _():
            z_copy(j, z - 1).wait_recv()

        @pl.when(z < nz - 1)
        def _():
            total = z_recv[j].astype(F32)
            for xs in range(nx):
                total = total + t_recv[xs, j].astype(F32)
            z_send[j] = total.astype(BF16)
            z_copy(j, z + 1).start()

        for xt in range(nx):

            @pl.when(xt != x)
            def _():
                running = z_recv[j].astype(F32)
                for xs in range(xt):
                    running = running + t_recv[xs, j].astype(F32)
                q_send[xt, j] = running.astype(BF16)
                q_copy(o, xt, j).start()

        for xt in range(nx):

            @pl.when(xt == x)
            def _():
                running = z_recv[j].astype(F32)
                for xs in range(xt):
                    running = running + t_recv[xs, j].astype(F32)
                deliver(o, running)

    def onward(j):
        for d in range(1, nx):
            o = lax.rem(x + d, nx) * hp + j
            q_copy(o, x, j).wait_recv()
            deliver(o, q_recv[o].astype(F32))

    def finish_head(head, prefix):
        at = lanes(head)
        n = numer[:, at] + jnp.dot(qphi[:, at], prefix, preferred_element_type=F32)
        mean = jnp.mean(n * n, axis=-1, keepdims=True)
        outv[:, at] = (n * lax.rsqrt(mean + 1e-06)).astype(BF16)

    def out_copy(head):
        at = lanes(head)
        return pltpu.make_async_copy(outv.at[:, at], o_hbm.at[:, at], out_sem.at[head])

    def finish(j):
        for d in range(nx):
            o = lax.rem(x + d, nx) * hp + j
            finish_head(c * HALF + o, p_own[o])
            out_copy(c * HALF + o).start()
            c_copy(o).wait_recv()
            finish_head(other * HALF + o, c_recv[o])
            out_copy(other * HALF + o).start()

    def relay_step(j, carry):
        chain(j)
        onward(j)

        @pl.when(early & (j > 0))
        def _():
            finish(j - 1)

        return carry

    lax.fori_loop(0, hp, relay_step, 0)

    @pl.when(early)
    def _():
        finish(hp - 1)

    @pl.when(jnp.logical_not(early))
    def _():
        local_all()

        def step(j, carry):
            finish(j)
            return carry

        lax.fori_loop(0, hp, step, 0)

    def drain(o, carry):
        e_copy(o).wait_send()
        c_copy(o).wait_send()
        out_copy(o).wait()
        out_copy(o + HALF).wait()
        return carry

    lax.fori_loop(0, HALF, drain, 0)

    def drain_first(t, carry):
        o, col, j = own_index(t)
        t_copy(o, col, j).wait_send()
        return carry

    lax.fori_loop(0, first_count, drain_first, 0)

    def drain_chain(j, carry):
        @pl.when(z < nz - 1)
        def _():
            z_copy(j, z + 1).wait_send()

        for d in range(1, nx):
            q_copy(x * hp + j, lax.rem(x + d, nx), j).wait_send()
        return carry

    lax.fori_loop(0, hp, drain_chain, 0)


def body(nx, nz, queries, keys, values):
    rows = queries.shape[0]
    hp = HALF // nx
    wide = pltpu.VMEM((rows, HEADS * HD), BF16)
    half = pltpu.VMEM((HALF, HD, HD), BF16)
    dma = pltpu.SemaphoreType.DMA
    return pl.pallas_call(
        functools.partial(kernel, nx, nz, hp, 4),
        out_shape=jax.ShapeDtypeStruct(queries.shape, BF16),
        in_specs=[pl.BlockSpec(memory_space=pl.ANY)] * 3,
        out_specs=pl.BlockSpec(memory_space=pl.ANY),
        scratch_shapes=[
            wide, wide, wide, wide, wide,
            pltpu.VMEM((rows, HEADS * HD), F32),
            wide,
            half, half, half, half,
            pltpu.VMEM((nx, hp, HD, HD), BF16),
            pltpu.VMEM((hp, HD, HD), BF16),
            pltpu.VMEM((hp, HD, HD), BF16),
            pltpu.VMEM((nx, hp, HD, HD), BF16),
            half, half, half, half,
            dma((4 * nx + 1,)), dma((HEADS,)),
            dma((HALF,)), dma((HALF,)),
            dma((HALF,)), dma((HALF,)),
            dma((hp,)), dma((hp,)),
            dma((HALF,)), dma((HALF,)),
            dma((HALF,)), dma((HALF,)),
        ],
        compiler_params=pltpu.CompilerParams(collective_id=0, has_side_effects=True),
    )(queries, keys, values)


def solution(mesh):
    spec = P(("parts", "ctx", "head", "sub"), None)
    return jax.shard_map(
        functools.partial(body, mesh.shape["head"], mesh.shape["ctx"]),
        mesh=mesh,
        in_specs=(spec, spec, spec),
        out_specs=spec,
        check_vma=False,
    )
```

time: 119 us -> 52.2 us (0.44)
  Pallas kernels: 0 us -> 49.3 us
  waiting for transfers between devices: 43 us -> 0 us
  blocking collectives: 16.5 us -> 0 us
  matrix products: 14.1 us -> 0 us
  starting transfers between devices: 13.8 us -> 0 us
  between operations: 13.5 us -> 0.01 us
  other arithmetic: 11 us -> 0 us
  local copies, waits for them, and re-layouts: 6.07 us -> 2.29 us
    pallas_call x0 -> x1, Pallas kernels: none -> 49.3 us  [body(): pl.pallas_call(functools.partial(kernel, nx, nz, hp, 4), out_shape=jax.Sh...]
    all_to_all x3 -> x0, waiting for transfers between devices: 33.3 us -> none  [the longest x1 12.2 us: body(): lax.all_to_all(phi_k, ('head', 'sub'), split_axis=1, concat_axis=0, tiled...]
    all_to_all x1 -> x0, blocking collectives: 16.5 us -> none  [body(): lax.all_to_all(scaled, ('head', 'sub'), split_axis=0, concat_axis=1, tile...]
    dot_general x5 -> x0, matrix products: 14.1 us -> none  [the longest x1 5.88 us: finish(): jnp.einsum('nbhd,nhde->nbhe', qb.astype(jnp.float32), earlier, precision=...]
    all_to_all x3 -> x0, starting transfers between devices: 13.8 us -> none  [the longest x1 5.19 us: body(): lax.all_to_all(phi_q, ('head', 'sub'), split_axis=1, concat_axis=0, tiled...]
    all_gather x1 -> x0, waiting for transfers between devices: 9.64 us -> none  [prefix_2(): gathered = lax.all_gather(array.astype(jnp.bfloat16), axis)]
    reshape x3 -> x0, local copies, waits for them, and re-layouts: 3.89 us -> none  [the longest x1 1.31 us: body(): phi_k = feature(keys).reshape(tok_rows, HEADS, HD)]
    add x3 -> x0, other arithmetic: 3.21 us -> none  [add_states(): return earlier + later]
  transfers between devices with their start and end apart: 4 -> 0, of which waited for: 4 -> 0; matrix products, arithmetic and copies ran while one was open for 12% -> 0% of each run, Pallas kernels for 0% -> 0%
where the time goes in v1:
time: 52.2 us; the launch traced here: 51.6 us
  Pallas kernels  49.3 us (94%)
  local copies, waits for them, and re-layouts  2.29 us (4%)
    pallas_call x1, Pallas kernels, body(): pl.pallas_call(functools.partial(kernel, nx, nz, hp, 4), out_shape=jax.Sh...  49.3 us
    unnamed x1, local copies, waits for them, and re-layouts  2.29 us

profile of v1, /device:TPU:29, one launch (start us, length us, event | category | flops | bytes accessed | tf_op | source)
XLA Modules:
  0.0 51.6 jit_solution(11475312683801019977)
XLA Ops:
  0.0 49.3 %shard_map.37 = bf16[128,4096]{1,0:T(8,128)(2,1)} custom-call(bf16[128,4096]{1,0:T(8,128)(2,1)} %q_hbm.1, bf16[128,4096]{1,0:T(8,128)(2,1)} %k_hbm.1, bf16[128,4096]{1,0:T(8,128)(2,1)} %v_hbm.1), custom_call_target="tpu_custom_call" | custom-call | tf_op jit(solution)/shard_map/pallas_call | solution.py:330
  49.3 2.3 %copy.5 = bf16[128,4096]{1,0:T(8,128)(2,1)} copy(bf16[128,4096]{1,0:T(8,128)(2,1)} %shard_map.37) | data formatting | bytes 2097152

commit v2 on v1

--- a/solution.py
+++ b/solution.py
@@ -25,7 +25,7 @@
 
 
 def kernel(
-    nx, nz, hp, lag,
+    nx, nz, hp, lag, wait_x, wait_c,
     q_hbm, k_hbm, v_hbm, o_hbm,
     qv, kv, vv, kphi, qphi, numer, outv,
     s_par, s_own, e1_recv, t_send, t_recv, z_send, z_recv, q_send, q_recv,
@@ -182,14 +182,10 @@
             numer[:, at] = jnp.dot(scores, vv[:, at], preferred_element_type=F32)
         return carry
 
-    def local_all():
-        lax.fori_loop(0, HEADS // 4, local_step, 0)
-
-    early = z >= (nz + 1) // 2
-
-    @pl.when(early)
-    def _():
-        local_all()
+    last = z == nz - 1
+    groups = HEADS // 4
+    before_relay = (groups * z) // max(nz - 1, 1)
+    lax.fori_loop(0, before_relay, local_step, 0)
 
     def deliver(o, before):
         @pl.when(c == 0)
@@ -268,24 +264,25 @@
             out_copy(other * HALF + o).start()
 
     def relay_step(j, carry):
-        chain(j)
-        onward(j)
-
-        @pl.when(early & (j > 0))
-        def _():
-            finish(j - 1)
-
-        return carry
-
-    lax.fori_loop(0, hp, relay_step, 0)
-
-    @pl.when(early)
+        @pl.when(j < hp)
+        def _():
+            chain(j)
+
+        @pl.when((j >= wait_x) & (j < hp + wait_x))
+        def _():
+            onward(j - wait_x)
+
+        @pl.when(last & (j >= wait_c))
+        def _():
+            finish(j - wait_c)
+
+        return carry
+
+    lax.fori_loop(0, hp + wait_c, relay_step, 0)
+
+    @pl.when(jnp.logical_not(last))
     def _():
-        finish(hp - 1)
-
-    @pl.when(jnp.logical_not(early))
-    def _():
-        local_all()
+        lax.fori_loop(before_relay, groups, local_step, 0)
 
         def step(j, carry):
             finish(j)
@@ -328,7 +325,7 @@
     half = pltpu.VMEM((HALF, HD, HD), BF16)
     dma = pltpu.SemaphoreType.DMA
     return pl.pallas_call(
-        functools.partial(kernel, nx, nz, hp, 4),
+        functools.partial(kernel, nx, nz, hp, 4, min(3, hp), min(4, hp)),
         out_shape=jax.ShapeDtypeStruct(queries.shape, BF16),
         in_specs=[pl.BlockSpec(memory_space=pl.ANY)] * 3,
         out_specs=pl.BlockSpec(memory_space=pl.ANY),

time: 52.2 us -> 34.7 us (0.66)
  the two profiles are of different devices: /device:TPU:29 before, /device:TPU:0 now
where the time goes in v2:
time: 34.7 us; the launch traced here: 34.6 us
  Pallas kernels  32.3 us (93%)
  local copies, waits for them, and re-layouts  2.29 us (7%)
    pallas_call x1, Pallas kernels, body(): pl.pallas_call(functools.partial(kernel, nx, nz, hp, 4, min(3, hp), min(4...  32.3 us
    unnamed x1, local copies, waits for them, and re-layouts  2.29 us

profile of v2, /device:TPU:0, one launch (start us, length us, event | category | flops | bytes accessed | tf_op | source)
XLA Modules:
  0.0 34.6 jit_solution(3596132660095048551)
XLA Ops:
  0.0 32.3 %shard_map.37 = bf16[128,4096]{1,0:T(8,128)(2,1)} custom-call(bf16[128,4096]{1,0:T(8,128)(2,1)} %q_hbm.1, bf16[128,4096]{1,0:T(8,128)(2,1)} %k_hbm.1, bf16[128,4096]{1,0:T(8,128)(2,1)} %v_hbm.1), custom_call_target="tpu_custom_call" | custom-call | tf_op jit(solution)/shard_map/pallas_call | solution.py:327
  32.3 2.3 %copy.5 = bf16[128,4096]{1,0:T(8,128)(2,1)} copy(bf16[128,4096]{1,0:T(8,128)(2,1)} %shard_map.37) | data formatting | bytes 2097152

commit v3 on v2

--- a/solution.py
+++ b/solution.py
@@ -25,7 +25,7 @@
 
 
 def kernel(
-    nx, nz, hp, lag, wait_x, wait_c,
+    nx, nz, hp, lag, wait_x, wait_c, unroll,
     q_hbm, k_hbm, v_hbm, o_hbm,
     qv, kv, vv, kphi, qphi, numer, outv,
     s_par, s_own, e1_recv, t_send, t_recv, z_send, z_recv, q_send, q_recv,
@@ -171,8 +171,8 @@
     causal = row >= colm
 
     def local_step(g, carry):
-        for i in range(4):
-            at = lanes(g * 4 + i)
+        for i in range(unroll):
+            at = lanes(g * unroll + i)
             pq = phi(qv[:, at])
             qphi[:, at] = pq
             scores = lax.dot_general(
@@ -183,7 +183,7 @@
         return carry
 
     last = z == nz - 1
-    groups = HEADS // 4
+    groups = HEADS // unroll
     before_relay = (groups * z) // max(nz - 1, 1)
     lax.fori_loop(0, before_relay, local_step, 0)
 
@@ -219,6 +219,8 @@
             z_send[j] = total.astype(BF16)
             z_copy(j, z + 1).start()
 
+    def back(j):
+        o = x * hp + j
         for xt in range(nx):
 
             @pl.when(xt != x)
@@ -255,20 +257,25 @@
         return pltpu.make_async_copy(outv.at[:, at], o_hbm.at[:, at], out_sem.at[head])
 
     def finish(j):
+        heads = []
         for d in range(nx):
             o = lax.rem(x + d, nx) * hp + j
-            finish_head(c * HALF + o, p_own[o])
-            out_copy(c * HALF + o).start()
             c_copy(o).wait_recv()
-            finish_head(other * HALF + o, c_recv[o])
-            out_copy(other * HALF + o).start()
+            heads.append((c * HALF + o, o, p_own))
+            heads.append((other * HALF + o, o, c_recv))
+        for head, o, held in heads:
+            finish_head(head, held[o])
+        for head, o, held in heads:
+            out_copy(head).start()
 
     def relay_step(j, carry):
-        @pl.when(j < hp)
-        def _():
-            chain(j)
-
-        @pl.when((j >= wait_x) & (j < hp + wait_x))
+        chain(j)
+
+        @pl.when(z > 0)
+        def _():
+            back(j)
+
+        @pl.when(last & (j >= wait_x))
         def _():
             onward(j - wait_x)
 
@@ -278,17 +285,30 @@
 
         return carry
 
-    lax.fori_loop(0, hp + wait_c, relay_step, 0)
-
-    @pl.when(jnp.logical_not(last))
+    lax.fori_loop(0, hp, relay_step, 0)
+
+    @pl.when(z == 0)
     def _():
-        lax.fori_loop(before_relay, groups, local_step, 0)
-
-        def step(j, carry):
-            finish(j)
+        def back_step(j, carry):
+            back(j)
             return carry
 
-        lax.fori_loop(0, hp, step, 0)
+        lax.fori_loop(0, hp, back_step, 0)
+
+    lax.fori_loop(before_relay, groups, local_step, 0)
+
+    def final_step(j, carry):
+        @pl.when(j < hp + wait_x)
+        def _():
+            onward(j - wait_x)
+
+        @pl.when(j >= wait_c)
+        def _():
+            finish(j - wait_c)
+
+        return carry
+
+    lax.fori_loop(jnp.where(last, hp, wait_x), hp + wait_c, final_step, 0)
 
     def drain(o, carry):
         e_copy(o).wait_send()
@@ -325,7 +345,7 @@
     half = pltpu.VMEM((HALF, HD, HD), BF16)
     dma = pltpu.SemaphoreType.DMA
     return pl.pallas_call(
-        functools.partial(kernel, nx, nz, hp, 4, min(3, hp), min(4, hp)),
+        functools.partial(kernel, nx, nz, hp, 4, min(4, hp), min(7, hp), 4),
         out_shape=jax.ShapeDtypeStruct(queries.shape, BF16),
         in_specs=[pl.BlockSpec(memory_space=pl.ANY)] * 3,
         out_specs=pl.BlockSpec(memory_space=pl.ANY),

time: 34.7 us -> 28.3 us (0.82)
  the two profiles are of different devices: /device:TPU:0 before, /device:TPU:29 now
where the time goes in v3:
time: 28.3 us; the launch traced here: 28.2 us
  Pallas kernels  25.9 us (92%)
  local copies, waits for them, and re-layouts  2.29 us (8%)
    pallas_call x1, Pallas kernels, body(): pl.pallas_call(functools.partial(kernel, nx, nz, hp, 4, min(4, hp), min(7...  25.9 us
    unnamed x1, local copies, waits for them, and re-layouts  2.29 us

profile of v3, /device:TPU:29, one launch (start us, length us, event | category | flops | bytes accessed | tf_op | source)
XLA Modules:
  0.0 28.2 jit_solution(9879502320255694855)
XLA Ops:
  0.0 25.9 %shard_map.37 = bf16[128,4096]{1,0:T(8,128)(2,1)} custom-call(bf16[128,4096]{1,0:T(8,128)(2,1)} %q_hbm.1, bf16[128,4096]{1,0:T(8,128)(2,1)} %k_hbm.1, bf16[128,4096]{1,0:T(8,128)(2,1)} %v_hbm.1), custom_call_target="tpu_custom_call" | custom-call | tf_op jit(solution)/shard_map/pallas_call | solution.py:347
  25.9 2.3 %copy.5 = bf16[128,4096]{1,0:T(8,128)(2,1)} copy(bf16[128,4096]{1,0:T(8,128)(2,1)} %shard_map.37) | data formatting | bytes 2097152

commit v4 on v3

--- a/solution.py
+++ b/solution.py
@@ -345,7 +345,7 @@
     half = pltpu.VMEM((HALF, HD, HD), BF16)
     dma = pltpu.SemaphoreType.DMA
     return pl.pallas_call(
-        functools.partial(kernel, nx, nz, hp, 4, min(4, hp), min(7, hp), 4),
+        functools.partial(kernel, nx, nz, hp, 4, min(5, hp), min(8, hp), 4),
         out_shape=jax.ShapeDtypeStruct(queries.shape, BF16),
         in_specs=[pl.BlockSpec(memory_space=pl.ANY)] * 3,
         out_specs=pl.BlockSpec(memory_space=pl.ANY),

time: 28.3 us -> 27.9 us (0.986)
  Pallas kernels: 25.9 us -> 25.5 us
    pallas_call x1, Pallas kernels: 25.9 us -> 25.5 us  [body(): pl.pallas_call(functools.partial(kernel, nx, nz, hp, 4, min(5, hp), min(8...]
where the time goes in v4:
time: 27.9 us; the launch traced here: 27.7 us
  Pallas kernels  25.5 us (91%)
  local copies, waits for them, and re-layouts  2.29 us (8%)
    pallas_call x1, Pallas kernels, body(): pl.pallas_call(functools.partial(kernel, nx, nz, hp, 4, min(5, hp), min(8...  25.5 us
    unnamed x1, local copies, waits for them, and re-layouts  2.29 us

profile of v4, /device:TPU:29, one launch (start us, length us, event | category | flops | bytes accessed | tf_op | source)
XLA Modules:
  0.0 27.7 jit_solution(4402003890424897411)
XLA Ops:
  0.0 25.5 %shard_map.37 = bf16[128,4096]{1,0:T(8,128)(2,1)} custom-call(bf16[128,4096]{1,0:T(8,128)(2,1)} %q_hbm.1, bf16[128,4096]{1,0:T(8,128)(2,1)} %k_hbm.1, bf16[128,4096]{1,0:T(8,128)(2,1)} %v_hbm.1), custom_call_target="tpu_custom_call" | custom-call | tf_op jit(solution)/shard_map/pallas_call | solution.py:347
  25.5 2.3 %copy.5 = bf16[128,4096]{1,0:T(8,128)(2,1)} copy(bf16[128,4096]{1,0:T(8,128)(2,1)} %shard_map.37) | data formatting | bytes 2097152
